TPU v7x, 32 devices: a whole 2x2x4 slice. The times are simulated.
32 devices in a mesh: dp: 8 (over y, x, core), fsdp: 4 (over z).
Axes of the slice: x: 2, y: 2, z: 4, core: 2. Of those that a mesh axis runs over, the one named last changes fastest.
Arguments:
- tokens: bfloat16 [46400, 1024], P(('dp', 'fsdp')), may hold values from -6 to 6
- output_grad: bfloat16 [46400, 1024], P(('dp', 'fsdp')), may hold values from -6 to 6
- group_member: int32 [8], P('dp'), may hold values from 0 to 1, as said below
- image_counts: int32 [2], replicated, may hold values from 64 to 4095
- position_source: int32 [145, 4], replicated, may hold values from 0 to 49
- position_table: bfloat16 [50, 1024], P(None, 'fsdp'), may hold values from -3 to 3
- first_gain: bfloat16 [1024], P('fsdp'), may hold values from 0.5 to 1.5
- first_shift: bfloat16 [1024], P('fsdp'), may hold values from -1 to 1
- input_proj: bfloat16 [1024, 3072], P('fsdp'), may hold values from -0.1875 to 0.1875
- query_bias: bfloat16 [1024], P('fsdp'), may hold values from -1 to 1
- value_bias: bfloat16 [1024], P('fsdp'), may hold values from -1 to 1
- output_proj: bfloat16 [1024, 1024], P('fsdp'), may hold values from -0.75 to 0.75
- output_bias: bfloat16 [1024], P('fsdp'), may hold values from -1 to 1
- second_gain: bfloat16 [1024], P('fsdp'), may hold values from 0.5 to 1.5
- second_shift: bfloat16 [1024], P('fsdp'), may hold values from -1 to 1
- hidden_weight: bfloat16 [1024, 4096], P('fsdp'), may hold values from -0.1875 to 0.1875
- hidden_bias: bfloat16 [4096], P('fsdp'), may hold values from -1 to 1
- return_weight: bfloat16 [4096, 1024], P('fsdp'), may hold values from -0.09375 to 0.09375
- return_bias: bfloat16 [1024], P('fsdp'), may hold values from -1 to 1
Outputs:
- block_out: bfloat16 [46400, 1024], P(('dp', 'fsdp'))
- tokens_grad: bfloat16 [46400, 1024], P(('dp', 'fsdp'))
- table_grad: float32 [50, 1024], P(None, 'fsdp')
- first_gain_grad: float32 [1024], P('fsdp')
- first_shift_grad: float32 [1024], P('fsdp')
- input_proj_grad: float32 [1024, 3072], P('fsdp')
- query_bias_grad: float32 [1024], P('fsdp')
- value_bias_grad: float32 [1024], P('fsdp')
- output_proj_grad: float32 [1024, 1024], P('fsdp')
- output_bias_grad: float32 [1024], P('fsdp')
- second_gain_grad: float32 [1024], P('fsdp')
- second_shift_grad: float32 [1024], P('fsdp')
- hidden_weight_grad: float32 [1024, 4096], P('fsdp')
- hidden_bias_grad: float32 [4096], P('fsdp')
- return_weight_grad: float32 [4096, 1024], P('fsdp')
- return_bias_grad: float32 [1024], P('fsdp')
Inputs may be any that keep to these rules, and one draw needn't show every extreme that they name: `group_member`: exactly 3 entries are 1, the others 0.
All inputs are finite; a program needn't handle non-finite values.
Results may differ from a plain program's by a relative error of at most 0.02.
Values may be sent and summed in bfloat16 or wider, within the bound.
No kernel may reach another device: no remote copies, remote signals or barrier semaphores. Data moves between devices by JAX's collectives and lax.ppermute only.
A program may use at most 320 MiB of HBM per device.

v0:
```python
from functools import partial
import math
import jax
import jax.numpy as jnp
from jax import lax
from jax.sharding import PartitionSpec as P

D = 1024
HEADS = 16
HEAD_DIM = 64
SG = 7
LG = 12
SMALL_LEN = 50
LARGE_LEN = 145
ROWS = 1450
EPS = 1e-06


def shortened(value):
    return jax.tree.map(lambda a: a.astype(jnp.bfloat16) if a.dtype == jnp.float32 else a, value)


def grid_fraction(index):
    scaled = jnp.maximum((2 * index + 1) * SG - LG, 0)
    lower = scaled // (2 * LG)
    return (scaled - 2 * LG * lower).astype(jnp.float32) / (2.0 * LG)


def interp_table(position_source):
    position = jnp.arange(LARGE_LEN, dtype=jnp.int32)
    patch = jnp.maximum(position - 1, 0)
    frac_row = grid_fraction(patch // LG)
    frac_col = grid_fraction(patch % LG)
    weights = jnp.stack(
        [
            (1.0 - frac_row) * (1.0 - frac_col),
            (1.0 - frac_row) * frac_col,
            frac_row * (1.0 - frac_col),
            frac_row * frac_col,
        ],
        axis=1,
    )
    class_row = (jnp.arange(4, dtype=jnp.int32) == 0).astype(jnp.float32)
    weights = jnp.where((position == 0)[:, None], class_row[None, :], weights)
    onehot = (
        position_source[:, :, None] == jnp.arange(SMALL_LEN, dtype=jnp.int32)[None, None, :]
    ).astype(jnp.float32)
    return jnp.sum(weights[:, :, None] * onehot, axis=1)


def layer_norm(values, gain, shift):
    average = jnp.mean(values, axis=-1, keepdims=True)
    centred = values - average
    variance = jnp.mean(centred * centred, axis=-1, keepdims=True)
    inv_std = lax.rsqrt(variance + EPS)
    normed = centred * inv_std
    return (normed * gain + shift, normed, inv_std)


def norm_back(grad_norm, normed, inv_std, gain):
    scaled = grad_norm * gain
    inner = (
        scaled
        - jnp.mean(scaled, axis=-1, keepdims=True)
        - normed * jnp.mean(scaled * normed, axis=-1, keepdims=True)
    )
    return (inv_std * inner, jnp.sum(grad_norm * normed, axis=0), jnp.sum(grad_norm, axis=0))


def image_scores(query_low, keys_low, length):
    images = ROWS // length
    query_img = query_low.reshape(images, length, HEADS, HEAD_DIM)
    keys_img = keys_low.reshape(images, length, HEADS, HEAD_DIM)
    logits = jnp.einsum("nqhd,nkhd->nhqk", query_img, keys_img, preferred_element_type=jnp.float32)
    return (logits / math.sqrt(HEAD_DIM), query_img, keys_img)


def attend_forward(query_low, keys_low, values_low, length):
    images = ROWS // length
    scores, _, _ = image_scores(query_low, keys_low, length)
    highest = jnp.max(scores, axis=-1, keepdims=True)
    log_total = highest + jnp.log(jnp.sum(jnp.exp(scores - highest), axis=-1, keepdims=True))
    probs = jnp.exp(scores - log_total)
    values_img = values_low.reshape(images, length, HEADS, HEAD_DIM)
    attended = jnp.einsum(
        "nhqk,nkhd->nqhd",
        probs.astype(jnp.bfloat16),
        values_img,
        preferred_element_type=jnp.float32,
    )
    lse_rows = jnp.transpose(log_total[..., 0], (0, 2, 1)).reshape(ROWS, HEADS)
    return (attended.reshape(ROWS, D).astype(jnp.bfloat16), lse_rows)


def attend_backward(query_low, keys_low, values_low, lse_rows, grad_att_low, length):
    images = ROWS // length
    scores, query_img, keys_img = image_scores(query_low, keys_low, length)
    log_total = jnp.transpose(lse_rows.reshape(images, length, HEADS), (0, 2, 1))[..., None]
    probs = jnp.exp(scores - log_total)
    values_img = values_low.reshape(images, length, HEADS, HEAD_DIM)
    grad_img = grad_att_low.reshape(images, length, HEADS, HEAD_DIM)
    grad_values = jnp.einsum(
        "nhqk,nqhd->nkhd", probs.astype(jnp.bfloat16), grad_img, preferred_element_type=jnp.float32
    )
    grad_probs = jnp.einsum(
        "nqhd,nkhd->nhqk", grad_img, values_img, preferred_element_type=jnp.float32
    )
    grad_scores = probs * (grad_probs - jnp.sum(grad_probs * probs, axis=-1, keepdims=True))
    grad_scores_low = grad_scores.astype(jnp.bfloat16)
    grad_query = jnp.einsum(
        "nhqk,nkhd->nqhd", grad_scores_low, keys_img, preferred_element_type=jnp.float32
    ) / math.sqrt(HEAD_DIM)
    grad_keys = jnp.einsum(
        "nhqk,nqhd->nkhd", grad_scores_low, query_img, preferred_element_type=jnp.float32
    ) / math.sqrt(HEAD_DIM)
    return (
        grad_query.reshape(ROWS, D).astype(jnp.bfloat16),
        grad_keys.reshape(ROWS, D).astype(jnp.bfloat16),
        grad_values.reshape(ROWS, D).astype(jnp.bfloat16),
    )


def per_device(
    tokens,
    output_grad,
    group_member,
    image_counts,
    position_source,
    position_table,
    first_gain,
    first_shift,
    input_proj,
    query_bias,
    value_bias,
    output_proj,
    output_bias,
    second_gain,
    second_shift,
    hidden_weight,
    hidden_bias,
    return_weight,
    return_bias,
):
    gathered = (
        lax.all_gather(input_proj, "fsdp", axis=0, tiled=True),
        lax.all_gather(output_proj, "fsdp", axis=0, tiled=True),
        lax.all_gather(hidden_weight, "fsdp", axis=0, tiled=True),
        lax.all_gather(return_weight, "fsdp", axis=0, tiled=True),
        lax.all_gather(first_gain, "fsdp", axis=0, tiled=True),
        lax.all_gather(first_shift, "fsdp", axis=0, tiled=True),
        lax.all_gather(query_bias, "fsdp", axis=0, tiled=True),
        lax.all_gather(value_bias, "fsdp", axis=0, tiled=True),
        lax.all_gather(output_bias, "fsdp", axis=0, tiled=True),
        lax.all_gather(second_gain, "fsdp", axis=0, tiled=True),
        lax.all_gather(second_shift, "fsdp", axis=0, tiled=True),
        lax.all_gather(hidden_bias, "fsdp", axis=0, tiled=True),
        lax.all_gather(return_bias, "fsdp", axis=0, tiled=True),
        lax.all_gather(position_table, "fsdp", axis=1, tiled=True),
    )
    (
        joint_proj,
        outproj_full,
        hidden_full,
        return_full,
        gain_one,
        shift_one,
        query_add,
        value_add,
        output_add,
        gain_two,
        shift_two,
        hidden_add,
        return_add,
        table_full,
    ) = gathered
    member = group_member[0]
    is_large = member == 1
    length = jnp.where(is_large, LARGE_LEN, SMALL_LEN)
    row_index = jnp.arange(ROWS, dtype=jnp.int32)
    place = row_index % length
    inter = interp_table(position_source)
    identity = (
        jnp.arange(LARGE_LEN, dtype=jnp.int32)[:, None]
        == jnp.arange(SMALL_LEN, dtype=jnp.int32)[None, :]
    ).astype(jnp.float32)
    mixing = jnp.where(is_large, inter, identity)
    picker = (place[:, None] == jnp.arange(LARGE_LEN, dtype=jnp.int32)[None, :]).astype(jnp.float32)
    spread = jnp.dot(picker, mixing, precision=lax.Precision.HIGHEST)
    position = jnp.dot(spread, table_full.astype(jnp.float32), precision=lax.Precision.HIGHEST)
    stream = tokens.astype(jnp.float32) + position
    first_out, first_hat, first_inv = layer_norm(
        stream, gain_one.astype(jnp.float32), shift_one.astype(jnp.float32)
    )
    first_low = first_out.astype(jnp.bfloat16)
    projected = jnp.dot(first_low, joint_proj, preferred_element_type=jnp.float32)
    query_low = (projected[:, :D] + query_add.astype(jnp.float32)).astype(jnp.bfloat16)
    keys_low = projected[:, D : 2 * D].astype(jnp.bfloat16)
    values_low = (projected[:, 2 * D :] + value_add.astype(jnp.float32)).astype(jnp.bfloat16)
    attended_low, lse_rows = lax.cond(
        is_large,
        partial(attend_forward, length=LARGE_LEN),
        partial(attend_forward, length=SMALL_LEN),
        query_low,
        keys_low,
        values_low,
    )
    mid = (
        stream
        + jnp.dot(attended_low, outproj_full, preferred_element_type=jnp.float32)
        + output_add.astype(jnp.float32)
    )
    second_out, second_hat, second_inv = layer_norm(
        mid, gain_two.astype(jnp.float32), shift_two.astype(jnp.float32)
    )
    second_low = second_out.astype(jnp.bfloat16)
    hidden_pre = jnp.dot(
        second_low, hidden_full, preferred_element_type=jnp.float32
    ) + hidden_add.astype(jnp.float32)
    activ, gelu_back = jax.vjp(partial(jax.nn.gelu, approximate=False), hidden_pre)
    activ_low = activ.astype(jnp.bfloat16)
    returned = jnp.dot(
        activ_low, return_full, preferred_element_type=jnp.float32
    ) + return_add.astype(jnp.float32)
    block_out = (mid + returned).astype(jnp.bfloat16)
    again = (
        lax.all_gather(input_proj, "fsdp", axis=0, tiled=True),
        lax.all_gather(output_proj, "fsdp", axis=0, tiled=True),
        lax.all_gather(hidden_weight, "fsdp", axis=0, tiled=True),
        lax.all_gather(return_weight, "fsdp", axis=0, tiled=True),
        lax.all_gather(first_gain, "fsdp", axis=0, tiled=True),
        lax.all_gather(second_gain, "fsdp", axis=0, tiled=True),
    )
    joint_back, outproj_back, hidden_back, return_back, gain_one_back, gain_two_back = again
    grad_out = output_grad.astype(jnp.float32)
    grad_return_w = jnp.einsum(
        "rf,rd->fd", activ_low, output_grad, preferred_element_type=jnp.float32
    )
    grad_return_add = jnp.sum(grad_out, axis=0)
    grad_activ = jnp.einsum(
        "rd,fd->rf", output_grad, return_back, preferred_element_type=jnp.float32
    )
    grad_hidden_low = gelu_back(grad_activ)[0].astype(jnp.bfloat16)
    grad_hidden_w = jnp.einsum(
        "rd,rf->df", second_low, grad_hidden_low, preferred_element_type=jnp.float32
    )
    grad_hidden_add = jnp.sum(grad_hidden_low.astype(jnp.float32), axis=0)
    grad_second = jnp.einsum(
        "rf,df->rd", grad_hidden_low, hidden_back, preferred_element_type=jnp.float32
    )
    grad_mid_norm, grad_gain_two, grad_shift_two = norm_back(
        grad_second, second_hat, second_inv, gain_two_back.astype(jnp.float32)
    )
    grad_mid = grad_out + grad_mid_norm
    grad_branch_low = grad_mid.astype(jnp.bfloat16)
    grad_outproj = jnp.einsum(
        "rd,re->de", attended_low, grad_branch_low, preferred_element_type=jnp.float32
    )
    grad_output_add = jnp.sum(grad_branch_low.astype(jnp.float32), axis=0)
    grad_attended = jnp.einsum(
        "re,de->rd", grad_branch_low, outproj_back, preferred_element_type=jnp.float32
    )
    grad_att_low = grad_attended.astype(jnp.bfloat16)
    grad_query_low, grad_keys_low, grad_values_low = lax.cond(
        is_large,
        partial(attend_backward, length=LARGE_LEN),
        partial(attend_backward, length=SMALL_LEN),
        query_low,
        keys_low,
        values_low,
        lse_rows,
        grad_att_low,
    )
    grad_joint_low = jnp.concatenate([grad_query_low, grad_keys_low, grad_values_low], axis=1)
    grad_joint = jnp.einsum(
        "rd,re->de", first_low, grad_joint_low, preferred_element_type=jnp.float32
    )
    grad_query_add = jnp.sum(grad_query_low.astype(jnp.float32), axis=0)
    grad_value_add = jnp.sum(grad_values_low.astype(jnp.float32), axis=0)
    grad_first = jnp.einsum(
        "re,de->rd", grad_joint_low, joint_back, preferred_element_type=jnp.float32
    )
    grad_stream_norm, grad_gain_one, grad_shift_one = norm_back(
        grad_first, first_hat, first_inv, gain_one_back.astype(jnp.float32)
    )
    grad_stream = grad_mid + grad_stream_norm
    tokens_grad = grad_stream.astype(jnp.bfloat16)
    grad_table = jnp.dot(spread.T, grad_stream, precision=lax.Precision.HIGHEST)
    dp_size = lax.axis_size("dp")
    fsdp_size = lax.axis_size("fsdp")
    group_high = dp_size * 7 // 16
    group_low = dp_size - group_high
    counts = image_counts.astype(jnp.float32)
    share = jnp.where(is_large, counts[1], counts[0]) / (counts[0] + counts[1])
    images = jnp.where(
        is_large,
        group_high * fsdp_size * (ROWS // LARGE_LEN),
        group_low * fsdp_size * (ROWS // SMALL_LEN),
    ).astype(jnp.float32)
    factor = share / images
    grads = (
        grad_joint,
        grad_outproj,
        grad_hidden_w,
        grad_return_w,
        grad_gain_one,
        grad_shift_one,
        grad_query_add,
        grad_value_add,
        grad_output_add,
        grad_gain_two,
        grad_shift_two,
        grad_hidden_add,
        grad_return_add,
        grad_table,
    )
    shares = (
        lax.psum_scatter(
            grads[0].astype(jnp.bfloat16), "fsdp", scatter_dimension=0, tiled=True
        ).astype(jnp.float32),
        lax.psum_scatter(
            grads[1].astype(jnp.bfloat16), "fsdp", scatter_dimension=0, tiled=True
        ).astype(jnp.float32),
        lax.psum_scatter(
            grads[2].astype(jnp.bfloat16), "fsdp", scatter_dimension=0, tiled=True
        ).astype(jnp.float32),
        lax.psum_scatter(
            grads[3].astype(jnp.bfloat16), "fsdp", scatter_dimension=0, tiled=True
        ).astype(jnp.float32),
        lax.psum_scatter(
            grads[4].astype(jnp.bfloat16), "fsdp", scatter_dimension=0, tiled=True
        ).astype(jnp.float32),
        lax.psum_scatter(
            grads[5].astype(jnp.bfloat16), "fsdp", scatter_dimension=0, tiled=True
        ).astype(jnp.float32),
        lax.psum_scatter(
            grads[6].astype(jnp.bfloat16), "fsdp", scatter_dimension=0, tiled=True
        ).astype(jnp.float32),
        lax.psum_scatter(
            grads[7].astype(jnp.bfloat16), "fsdp", scatter_dimension=0, tiled=True
        ).astype(jnp.float32),
        lax.psum_scatter(
            grads[8].astype(jnp.bfloat16), "fsdp", scatter_dimension=0, tiled=True
        ).astype(jnp.float32),
        lax.psum_scatter(
            grads[9].astype(jnp.bfloat16), "fsdp", scatter_dimension=0, tiled=True
        ).astype(jnp.float32),
        lax.psum_scatter(
            grads[10].astype(jnp.bfloat16), "fsdp", scatter_dimension=0, tiled=True
        ).astype(jnp.float32),
        lax.psum_scatter(
            grads[11].astype(jnp.bfloat16), "fsdp", scatter_dimension=0, tiled=True
        ).astype(jnp.float32),
        lax.psum_scatter(
            grads[12].astype(jnp.bfloat16), "fsdp", scatter_dimension=0, tiled=True
        ).astype(jnp.float32),
        lax.psum_scatter(
            grads[13].astype(jnp.bfloat16), "fsdp", scatter_dimension=1, tiled=True
        ).astype(jnp.float32),
    )
    merged = jax.tree.map(
        lambda part: part.astype(jnp.float32),
        lax.psum(shortened(tuple((piece * factor for piece in shares))), "dp"),
    )
    return (
        block_out,
        tokens_grad,
        merged[13],
        merged[4],
        merged[5],
        merged[0],
        merged[6],
        merged[7],
        merged[1],
        merged[8],
        merged[9],
        merged[10],
        merged[2],
        merged[11],
        merged[3],
        merged[12],
    )


def solution(mesh):
    in_specs = (
        P(("dp", "fsdp"), None),
        P(("dp", "fsdp"), None),
        P("dp"),
        P(),
        P(),
        P(None, "fsdp"),
        P("fsdp"),
        P("fsdp"),
        P("fsdp", None),
        P("fsdp"),
        P("fsdp"),
        P("fsdp", None),
        P("fsdp"),
        P("fsdp"),
        P("fsdp"),
        P("fsdp", None),
        P("fsdp"),
        P("fsdp", None),
        P("fsdp"),
    )
    out_specs = (
        P(("dp", "fsdp"), None),
        P(("dp", "fsdp"), None),
        P(None, "fsdp"),
        P("fsdp"),
        P("fsdp"),
        P("fsdp", None),
        P("fsdp"),
        P("fsdp"),
        P("fsdp", None),
        P("fsdp"),
        P("fsdp"),
        P("fsdp"),
        P("fsdp", None),
        P("fsdp"),
        P("fsdp", None),
        P("fsdp"),
    )
    return jax.shard_map(
        per_device, mesh=mesh, in_specs=in_specs, out_specs=out_specs, check_vma=False
    )
```

profile of v0, /device:TPU:0, one launch (start us, length us, event | category | flops | bytes accessed | tf_op | source)
XLA Modules:
  0.0 1341.7 jit_solution(7933301942073396000)
XLA Ops:
  11.0 12.6 all-gather.6
  31.4 9.9 all-gather.4
  41.2 9.6 all-gather.3
  50.9 8.5 all-gather.2
  59.4 10.3 all-gather.1
  69.7 8.6 all-gather
  78.5 12.1 all_gather.59
  90.6 16.1 %all_gather.48 = bf16[50,1024]{1,0:T(8,128)(2,1)S(1)} all-gather(bf16[50,256]{1,0:T(8,128)(2,1)S(1)} %copy-done.33), channel_id=1, replica_groups=mesh['dp'=8,'fsdp'=4] {'fsdp'}, dimensions={1}, use_global_device_ids=true | all-gather | bytes 128000 | tf_op jit(solution)/shard_map/all_gather | solution.py:158
  114.2 15.8 %all-gather.13.cloned.1.call-done = bf16[1024,3072]{1,0:T(8,128)(2,1)} async-done(((bf16[256,3072]{1,0:T(8,128)(2,1)}), bf16[1024,3072]{1,0:T(8,128)(2,1)}) %all-gather.13.cloned.1.call-update) | async-done | bytes 6291472 | tf_op jit(solution)/shard_map/all_gather | solution.py:145
  130.0 17.1 %fusion.72 = f32[1450,3072]{1,0:T(8,128)} fusion(bf16[1024,3072]{1,0:T(8,128)(2,1)} %all-gather.13.cloned.1.call-done, f32[1450,1024]{1,0:T(8,128)} %copy-done.7, f32[1024]{0:T(1024)S(1)} %bitcast.103, f32[1024]{0:T(1024)S(1)} %bitcast.95, f32[1450]{0:T(1024)S(1)} %add_rsqrt_fusion.1, f32[1450]{0:T(1024)S(1)} %broadcast_multiply_fusion.5), kind=kOutput, calls=%fused_computation.164 | convolution fusion | flops 9130035200 | bytes 30068048 | tf_op jit(solution)/shard_map/dot_general | solution.py:195
  150.3 10.0 fusion.50
  160.3 75.3 %conditional.6 = (f32[1450,16]{0,1:T(8,128)}, bf16[1450,1024]{1,0:T(8,128)(2,1)S(1)}) conditional(s32[]{:T(128)} %convert_element_type.404, (bf16[1450,1024]{1,0:T(8,128)(2,1)}, bf16[1450,1024]{1,0:T(8,128)(2,1)S(1)}, bf16[1450,1024]{1,0:T(8,128)(2,1)}) %tuple.44, (bf16[1450,1024]{1,0:T(8,128)(2,1)}, bf16[1450,1024]{1,0:T(8,128)(2,1)S(1)}, ...), branch_computations={%region_3.6_spmd, %region_6.9_spmd} | conditional | flops 889557632 | bytes 82963216
  160.3 8.9 reshape.396
  175.4 14.4 %multiply_reduce_fusion = (f32[29,16,50]{2,1,0:T(8,128)S(1)}, f32[29,16,50,50]{2,3,1,0:T(8,128)}) fusion(bf16[29,50,16,64]{3,2,1,0:T(8,128)(2,1)} %reshape.397, bf16[29,50,16,64]{3,2,1,0:T(8,128)(2,1)} %reshape.396), kind=kOutput, calls=%fused_computation.2 | convolution fusion | flops 150776800 | bytes 10672000 | tf_op jit(solution)/shard_map/cond/branch_0_fun/nqhd,nkhd->nhqk/dot_general | solution.py:74
  189.8 8.9 exponential_reduce_fusion
  206.3 8.9 fusion.6
  218.6 7.8 convert_element_type.297
  246.5 79.2 %all-gather.17.cloned.1.call-done = bf16[1024,4096]{1,0:T(8,128)(2,1)} async-done(((bf16[256,4096]{1,0:T(8,128)(2,1)}), bf16[1024,4096]{1,0:T(8,128)(2,1)}) %all-gather.17.cloned.1.call-update) | async-done | bytes 8388624 | tf_op jit(solution)/shard_map/all_gather | solution.py:147
  325.7 70.6 %multiply_convert_fusion.4 = (bf16[1450,4096]{1,0:T(8,128)(2,1)}, f32[1450,4096]{1,0:T(8,128)}, f32[1450,4096]{1,0:T(8,128)}) fusion(f32[4096]{0:T(1024)S(1)} %convert_element_type.416, bf16[1024,4096]{1,0:T(8,128)(2,1)} %all-gather.17.cloned.1.call-done, f32[1450,1024]{1,0:T(8,128)} %copy-done.8, f32[1024]{0:T(1024)S(1)} %bitcast.101, ...), kind=kOutput, calls=%fused_computation.59 | convolution fusion | flops 12562892800 | bytes 73755984 | tf_op jit(solution)/shard_map/dot_general | solution.py:216
  396.3 78.7 %all-gather.19.cloned.1.call-done = bf16[4096,1024]{1,0:T(8,128)(2,1)} async-done(((bf16[1024,1024]{1,0:T(8,128)(2,1)}), bf16[4096,1024]{1,0:T(8,128)(2,1)}) %all-gather.19.cloned.1.call-update) | async-done | bytes 8388624 | tf_op jit(solution)/shard_map/all_gather | solution.py:148
  475.0 32.7 %fusion.79 = (bf16[4096]{0:T(1024)(128)(2,1)}, bf16[1450,4096]{1,0:T(8,128)(2,1)}) fusion(f32[1450,4096]{1,0:T(8,128)} %get-tuple-element.140, bf16[1450,1024]{1,0:T(8,128)(2,1)} %param.24, bf16[4096,1024]{1,0:T(8,128)(2,1)} %all-gather.19.cloned.1.call-done, f32[1450,4096]{1,0:T(8,128)} %get-tuple-element.158, f32[4096]{0:T(1024)S(1)} %convert_element_type.416), kind=kOutput, calls=%fused_computation.170 | convolution fusion | flops 12258504704 | bytes 70774784 | tf_op jit(solution)/shard_map/rd,fd->rf/dot_general | solution.py:239
  507.7 22.8 %multiply_reduce_fusion.4 = (bf16[1024]{0:T(1024)(128)(2,1)}, f32[1450]{0:T(1024)S(1)}, f32[1450]{0:T(1024)S(1)}, bf16[1024]{0:T(1024)(128)(2,1)}, f32[1450,1024]{1,0:T(8,128)}) fusion(f32[1450,1024]{1,0:T(8,128)S(1)} %copy-done.9, f32[1450]{0:T(1024)S(1)} %add_rsqrt_fusion, f32[1450]{0:T(1024)S(1)} %broadcast_multiply_fusion.4, f32[1024]{0:T(1024)S(1)} %bitcast.92, ...), kind=kOutput, calls=%fused_computation.81 | convolution fusion | flops 12176840704 | bytes 32176800 | tf_op jit(solution)/shard_map/rf,df->rd/dot_general | solution.py:247
  544.0 8.4 convolution_convert_fusion.4
  552.4 154.3 %conditional.7 = (bf16[1450,1024]{1,0:T(8,128)(2,1)S(1)}, bf16[1450,1024]{1,0:T(8,128)(2,1)}, bf16[1450,1024]{1,0:T(8,128)(2,1)}) conditional(s32[]{:T(128)} %convert_element_type.404, (bf16[1450,1024]{1,0:T(8,128)(2,1)}, bf16[1450,1024]{1,0:T(8,128)(2,1)S(1)}, f32[1450,16]{0,1:T(8,128)S(1)}, bf16[1450,1024]{1,0:T(8,128)(2,1)}, ...), branch_computations={%region_13.15_spmd, %region_15.17_spmd} | conditional | flops 2199244032 | bytes 259700960
  552.9 8.7 reshape.404
  567.9 9.3 reshape.407
  583.4 13.5 %subtract_exponential_fusion = f32[29,16,50,50]{2,3,1,0:T(8,128)} fusion(f32[29,16,50]{2,1,0:T(8,128)S(1)} %copy.163, bf16[29,50,16,64]{3,2,1,0:T(8,128)(2,1)} %reshape.405, bf16[29,50,16,64]{3,2,1,0:T(8,128)(2,1)} %reshape.404), kind=kOutput, calls=%fused_computation.30 | convolution fusion | flops 150800000 | bytes 10672000 | tf_op jit(solution)/shard_map/cond/branch_0_fun/nqhd,nkhd->nhqk/dot_general | solution.py:74
  597.0 8.4 convolution_bitcast_fusion
  608.8 8.9 reshape.410
  617.7 14.1 %multiply_reduce_fusion.2 = (f32[29,16,50]{2,1,0:T(8,128)S(1)}, f32[29,16,50,50]{2,3,1,0:T(8,128)}) fusion(f32[29,16,50,50]{2,3,1,0:T(8,128)} %subtract_exponential_fusion, bf16[29,50,16,64]{3,2,1,0:T(8,128)(2,1)} %reshape.408, bf16[29,50,16,64]{3,2,1,0:T(8,128)(2,1)} %reshape.407), kind=kOutput, calls=%fused_computation.29 | convolution fusion | flops 150776800 | bytes 15312000 | tf_op jit(solution)/shard_map/cond/branch_0_fun/nqhd,nkhd->nhqk/dot_general | solution.py:105
  631.8 9.8 multiply_convert_fusion.1
  644.5 9.1 fusion.29
  653.6 11.0 multiply_bitcast_fusion
  671.0 7.8 reshape.409
  685.1 8.9 convert_element_type.306
  706.8 18.2 %convolution_convert_fusion.3 = bf16[1024,3072]{1,0:T(8,128)(2,1)} fusion(bf16[1450,1024]{1,0:T(8,128)(2,1)} %get-tuple-element.93, bf16[1450,1024]{1,0:T(8,128)(2,1)} %get-tuple-element.92, bf16[1450,1024]{1,0:T(8,128)(2,1)S(1)} %get-tuple-element.91, f32[1450,1024]{1,0:T(8,128)} %copy-done.7, f32[1024]{0:T(1024)S(1)} %bitcast.104, f32[1024]{0:T(1024)S(1)} %bitcast.96, ...), kind=kOutput, calls=%fused_computation.94 | convolution fusion | flops 9159907328 | bytes 21159248 | tf_op jit(solution)/shard_map/rd,re->de/dot_general | solution.py:274
  725.7 21.0 %convolution_convert_fusion.1 = bf16[1024,4096]{1,0:T(8,128)(2,1)} fusion(bf16[1450,4096]{1,0:T(8,128)(2,1)} %get-tuple-element.162, f32[1450,1024]{1,0:T(8,128)} %copy-done.8, f32[1024]{0:T(1024)S(1)} %bitcast.102, f32[1024]{0:T(1024)S(1)} %bitcast.94, f32[1450]{0:T(1024)S(1)} %copy-done.32, f32[1450]{0:T(1024)S(1)} %copy-done.28), kind=kOutput, calls=%fused_computation.74 | convolution fusion | flops 12175099904 | bytes 26226000 | tf_op jit(solution)/shard_map/rd,rf->df/dot_general | solution.py:243
  748.6 18.5 %convolution_convert_fusion.2 = bf16[4096,1024]{1,0:T(8,128)(2,1)} fusion(bf16[1450,4096]{1,0:T(8,128)(2,1)} %get-tuple-element.139, bf16[1450,1024]{1,0:T(8,128)(2,1)S(1)} %copy-done.17), kind=kOutput, calls=%fused_computation.75 | convolution fusion | flops 12167675904 | bytes 23236608 | tf_op jit(solution)/shard_map/rf,rd->fd/dot_general | solution.py:235
  772.8 7.9 all-gather.7
  783.7 18.3 %multiply_reduce_fusion.5 = (bf16[1024]{0:T(1024)(128)(2,1)S(1)}, f32[1450]{0:T(1024)S(1)}, f32[1450]{0:T(1024)S(1)}, bf16[1024]{0:T(1024)(128)(2,1)S(1)}, f32[1450,1024]{1,0:T(8,128)}) fusion(f32[1450,1024]{1,0:T(8,128)} %copy-done.7, f32[1450]{0:T(1024)S(1)} %copy-done.30, f32[1450]{0:T(1024)S(1)} %copy-done.26, f32[1024]{0:T(1024)S(1)} %bitcast.97, ...), kind=kOutput, calls=%fused_computation.82 | convolution fusion | flops 9162696704 | bytes 27110048 | tf_op jit(solution)/shard_map/re,de->rd/dot_general | solution.py:279
  802.0 21.2 %all-reduce.11 = (bf16[1024]{0:T(1024)(128)(2,1)S(1)}, bf16[1024]{0:T(1024)(128)(2,1)S(1)}, bf16[1024]{0:T(1024)(128)(2,1)S(1)}, bf16[1024]{0:T(1024)(128)(2,1)S...) all-reduce(bf16[1024]{0:T(1024)(128)(2,1)S(1)} %get-tuple-element.1, ...), channel_id=3, replica_groups=mesh['dp'=8,'fsdp'=4] {'fsdp'}, use_global_device_ids=true, to_apply=%region_22.23.clone | all-reduce | flops 12288 | bytes 49152
  823.9 8.9 fusion.74
  839.2 58.6 %reduce-scatter.8.cloned.1.call-done = bf16[256,3072]{1,0:T(8,128)(2,1)} async-done(((bf16[1024,3072]{1,0:T(8,128)(2,1)}), bf16[256,3072]{1,0:T(8,128)(2,1)}) %reduce-scatter.8.cloned.1.call-update) | async-done | bytes 1572880 | tf_op jit(solution)/shard_map/reduce_scatter | solution.py:317
  900.6 144.6 %reduce-scatter.12.cloned.1.call-done = bf16[256,4096]{1,0:T(8,128)(2,1)} async-done(((bf16[1024,4096]{1,0:T(8,128)(2,1)}), bf16[256,4096]{1,0:T(8,128)(2,1)}) %reduce-scatter.12.cloned.1.call-update) | async-done | bytes 2097168 | tf_op jit(solution)/shard_map/reduce_scatter | solution.py:323
  1048.6 144.4 %reduce-scatter.14.cloned.1.call-done = bf16[1024,1024]{1,0:T(8,128)(2,1)} async-done(((bf16[4096,1024]{1,0:T(8,128)(2,1)}), bf16[1024,1024]{1,0:T(8,128)(2,1)}) %reduce-scatter.14.cloned.1.call-update) | async-done | bytes 2097168 | tf_op jit(solution)/shard_map/reduce_scatter | solution.py:326
  1196.4 19.1 %add_convert_fusion.1 = bf16[1450,1024]{1,0:T(8,128)(2,1)} fusion(f32[1450,1024]{1,0:T(8,128)} %copy-done.8, bf16[1450,4096]{1,0:T(8,128)(2,1)} %get-tuple-element.139, bf16[4096,1024]{1,0:T(8,128)(2,1)} %all-gather.19.cloned.1.call-done, f32[1024]{0:T(1024)S(1)} %bitcast.106), kind=kOutput, calls=%fused_computation.87 | convolution fusion | flops 12167936000 | bytes 29179904 | tf_op jit(solution)/shard_map/dot_general | solution.py:221
  1216.3 25.7 %all-reduce.9 = (bf16[50,256]{1,0:T(8,128)(2,1)S(1)}, bf16[256]{0:T(256)(128)(2,1)S(1)}, bf16[256]{0:T(256)(128)(2,1)S(1)}, bf16[256]{0:T(256)(128)(2,1)S(1)}, b...) all-reduce(bf16[50,256]{1,0:T(8,128)(2,1)S(1)} %multiply_convert_fu, ...), channel_id=1, replica_groups=mesh['dp'=8,'fsdp'=4] {'dp'}, use_global_device_ids=true, to_apply=%region_20.21 | all-reduce | flops 15872 | bytes 63488 | tf_op jit(solution)/shard_map/psum | solution.py:362
  1247.7 75.9 %all-reduce.14.cloned.1.call-done = (bf16[256,3072]{1,0:T(8,128)(2,1)}, bf16[256,1024]{1,0:T(8,128)(2,1)}, bf16[256,4096]{1,0:T(8,128)(2,1)}, bf16[1024,1024]{1,0:T(8,128)(2,1)}) async-done(((bf16[256,3072]{1,0:T(8,128)(2,1)}, bf16[256,1024]{1,0:T(8,128)(2,1)}, bf16[256,4096]{1,0:T(8,128)(2,1)}, bf16[1024,1024]{1,0:T(8,128)(2,1)}), (bf16[256,3072]{1,0:T(8,128)(2,1)}, bf16[256,1024]{1,0:T(8,128)(2,1)}, ...) | async-done | bytes 6291472 | tf_op jit(solution)/shard_map/psum | solution.py:362
  (221 shorter events, 135.7 us)
Async XLA Ops:
  7.2 3.8 copy-start.55
  7.3 71.3 %copy-start.46 = (bf16[1024]{0:T(1024)(128)(2,1)S(1)}, bf16[1024]{0:T(1024)(128)(2,1)}, u32[]{:S(2)}) copy-start(bf16[1024]{0:T(1024)(128)(2,1)} %param.39) | copy-start | bytes 6148
  7.3 83.3 %copy-start.33 = (bf16[50,256]{1,0:T(8,128)(2,1)S(1)}, bf16[50,256]{1,0:T(8,128)(2,1)}, u32[]{:S(2)}) copy-start(bf16[50,256]{1,0:T(8,128)(2,1)} %param.28) | copy-start | bytes 76804
  7.3 99.5 %copy-start.41 = (s32[145,4]{0,1:T(4,128)S(1)}, s32[145,4]{0,1:T(4,128)}, u32[]{:S(2)}) copy-start(s32[145,4]{0,1:T(4,128)} %param.27) | copy-start | bytes 6964
  7.3 100.5 %copy-start.18 = (bf16[1450,1024]{1,0:T(8,128)(2,1)S(1)}, bf16[1450,1024]{1,0:T(8,128)(2,1)}, u32[]{:S(2)}) copy-start(bf16[1450,1024]{1,0:T(8,128)(2,1)} %param.23) | copy-start | bytes 8908804
  7.3 122.7 %all-gather.13.cloned.1.call-start = ((), (), s32[]{:S(2)}) async-start(), calls=%async_computation.5 | async-start | bytes 7864320 | tf_op jit(solution)/shard_map/all_gather | solution.py:145
  8.0 227.7 %all-gather.15.cloned.1.call-start = ((), (), s32[]{:S(2)}) async-start(), calls=%async_computation.6 | async-start | bytes 2621440 | tf_op jit(solution)/shard_map/all_gather | solution.py:146
  8.8 316.9 %all-gather.17.cloned.1.call-start = ((), (), s32[]{:S(2)}) async-start(), calls=%async_computation.7 | async-start | bytes 10485760 | tf_op jit(solution)/shard_map/all_gather | solution.py:147
  9.5 465.5 %all-gather.19.cloned.1.call-start = ((), (), s32[]{:S(2)}) async-start(), calls=%async_computation.8 | async-start | bytes 10485760 | tf_op jit(solution)/shard_map/all_gather | solution.py:148
  10.1 827.2 %reduce-scatter.10.cloned.1.call-start = ((), (), s32[]{:S(2)}) async-start(), calls=%async_computation.11 | async-start | bytes 2621440 | tf_op jit(solution)/shard_map/reduce_scatter | solution.py:320
  23.7 302.0 %copy-start.42 = (f32[4,1,256]{2,1,0:T(1,128)}, f32[4,1,256]{2,1,0:T(1,128)S(1)}, u32[]{:S(2)}) copy-start(f32[4,1,256]{2,1,0:T(1,128)S(1)} %convert_element_type.486) | copy-start | bytes 12292
  31.4 499.1 %copy-start.34 = (f32[4,1,256]{2,1,0:T(1,128)}, f32[4,1,256]{2,1,0:T(1,128)S(1)}, u32[]{:S(2)}) copy-start(f32[4,1,256]{2,1,0:T(1,128)S(1)} %convert_element_type.485) | copy-start | bytes 12292
  69.7 60.2 %copy-start.44 = (f32[4,1,256]{2,1,0:T(1,128)}, f32[4,1,256]{2,1,0:T(1,128)S(1)}, u32[]{:S(2)}) copy-start(f32[4,1,256]{2,1,0:T(1,128)S(1)} %convert_element_type.481) | copy-start | bytes 12292
  78.4 51.6 %copy-start.36 = (f32[4,1,256]{2,1,0:T(1,128)}, f32[4,1,256]{2,1,0:T(1,128)S(1)}, u32[]{:S(2)}) copy-start(f32[4,1,256]{2,1,0:T(1,128)S(1)} %convert_element_type.480) | copy-start | bytes 12292
  111.0 19.0 %copy-start.25 = (f32[1450]{0:T(1024)}, f32[1450]{0:T(1024)S(1)}, u32[]{:S(2)}) copy-start(f32[1450]{0:T(1024)S(1)} %broadcast_multiply_fusion.5) | copy-start | bytes 17404
  114.2 15.8 %copy-start.29 = (f32[1450]{0:T(1024)}, f32[1450]{0:T(1024)S(1)}, u32[]{:S(2)}) copy-start(f32[1450]{0:T(1024)S(1)} %add_rsqrt_fusion.1) | copy-start | bytes 17404
  150.3 10.0 copy-start.1
  189.8 10.3 copy-start.3
  235.6 7.5 copy-start.14
  243.2 287.2 %copy-start.27 = (f32[1450]{0:T(1024)}, f32[1450]{0:T(1024)S(1)}, u32[]{:S(2)}) copy-start(f32[1450]{0:T(1024)S(1)} %broadcast_multiply_fusion.4) | copy-start | bytes 17404
  246.5 284.0 %copy-start.31 = (f32[1450]{0:T(1024)}, f32[1450]{0:T(1024)S(1)}, u32[]{:S(2)}) copy-start(f32[1450]{0:T(1024)S(1)} %add_rsqrt_fusion) | copy-start | bytes 17404
  475.0 32.7 %copy-start.9 = (f32[1450,1024]{1,0:T(8,128)S(1)}, f32[1450,1024]{1,0:T(8,128)}, u32[]{:S(2)}) copy-start(f32[1450,1024]{1,0:T(8,128)} %copy-done.8) | copy-start | bytes 17817604
  507.7 22.8 %copy-start.16 = (bf16[1450,1024]{1,0:T(8,128)(2,1)S(1)}, bf16[1450,1024]{1,0:T(8,128)(2,1)}, u32[]{:S(2)}) copy-start(bf16[1450,1024]{1,0:T(8,128)(2,1)} %param.24) | copy-start | bytes 8908804
  530.5 8.7 copy-start.15
  544.0 8.5 copy-start.2
  544.0 8.4 copy-start.23
  544.0 353.8 %reduce-scatter.8.cloned.1.call-start = ((), (), s32[]{:S(2)}) async-start(), calls=%async_computation.10 | async-start | bytes 7864320 | tf_op jit(solution)/shard_map/reduce_scatter | solution.py:317
  552.4 154.4 %copy-start.26 = (f32[1450]{0:T(1024)S(1)}, f32[1450]{0:T(1024)}, u32[]{:S(2)}) copy-start(f32[1450]{0:T(1024)} %copy-done.25) | copy-start | bytes 17404
  552.4 154.4 %copy-start.30 = (f32[1450]{0:T(1024)S(1)}, f32[1450]{0:T(1024)}, u32[]{:S(2)}) copy-start(f32[1450]{0:T(1024)} %copy-done.29) | copy-start | bytes 17404
  552.4 154.4 %copy-start.37 = (f32[4,1,256]{2,1,0:T(1,128)S(1)}, f32[4,1,256]{2,1,0:T(1,128)}, u32[]{:S(2)}) copy-start(f32[4,1,256]{2,1,0:T(1,128)} %copy-done.36) | copy-start | bytes 12292
  552.4 154.4 %copy-start.45 = (f32[4,1,256]{2,1,0:T(1,128)S(1)}, f32[4,1,256]{2,1,0:T(1,128)}, u32[]{:S(2)}) copy-start(f32[4,1,256]{2,1,0:T(1,128)} %copy-done.44) | copy-start | bytes 12292
  567.9 9.3 copy-start.4
  706.8 18.3 %copy-start.13 = (bf16[1450,1024]{1,0:T(8,128)(2,1)}, bf16[1450,1024]{1,0:T(8,128)(2,1)S(1)}, u32[]{:S(2)}) copy-start(bf16[1450,1024]{1,0:T(8,128)(2,1)S(1)} %get-tuple-element.91) | copy-start | bytes 8908804
  725.1 320.2 %reduce-scatter.12.cloned.1.call-start = ((), (), s32[]{:S(2)}) async-start(), calls=%async_computation.12 | async-start | bytes 10485760 | tf_op jit(solution)/shard_map/reduce_scatter | solution.py:323
  746.8 446.2 %reduce-scatter.14.cloned.1.call-start = ((), (), s32[]{:S(2)}) async-start(), calls=%async_computation.13 | async-start | bytes 10485760 | tf_op jit(solution)/shard_map/reduce_scatter | solution.py:326
  767.0 3.8 copy-start.58
  767.0 5.7 copy-start.57
  767.0 16.1 %copy-start.12 = (bf16[1450,1024]{1,0:T(8,128)(2,1)S(1)}, bf16[1450,1024]{1,0:T(8,128)(2,1)}, u32[]{:S(2)}) copy-start(bf16[1450,1024]{1,0:T(8,128)(2,1)} %get-tuple-element.93) | copy-start | bytes 8908804
  767.1 448.4 %reduce-scatter.6.cloned.1.call-start = ((), (), s32[]{:S(2)}) async-start(), calls=%async_computation.9 | async-start | bytes 143360 | tf_op jit(solution)/shard_map/reduce_scatter | solution.py:356
  783.7 18.3 %copy-start.38 = (bf16[1024]{0:T(1024)(128)(2,1)S(1)}, bf16[1024]{0:T(1024)(128)(2,1)}, u32[]{:S(2)}) copy-start(bf16[1024]{0:T(1024)(128)(2,1)} %get-tuple-element.135) | copy-start | bytes 6148
  783.7 18.3 %copy-start.39 = (bf16[1024]{0:T(1024)(128)(2,1)S(1)}, bf16[1024]{0:T(1024)(128)(2,1)}, u32[]{:S(2)}) copy-start(bf16[1024]{0:T(1024)(128)(2,1)} %get-tuple-element.151) | copy-start | bytes 6148
  783.7 18.3 %copy-start.40 = (bf16[4096]{0:T(1024)(128)(2,1)S(1)}, bf16[4096]{0:T(1024)(128)(2,1)}, u32[]{:S(2)}) copy-start(bf16[4096]{0:T(1024)(128)(2,1)} %get-tuple-element.161) | copy-start | bytes 24580
  783.7 18.3 %copy-start.47 = (bf16[1024]{0:T(1024)(128)(2,1)S(1)}, bf16[1024]{0:T(1024)(128)(2,1)}, u32[]{:S(2)}) copy-start(bf16[1024]{0:T(1024)(128)(2,1)} %get-tuple-element.104) | copy-start | bytes 6148
  783.7 18.3 %copy-start.48 = (bf16[1024]{0:T(1024)(128)(2,1)S(1)}, bf16[1024]{0:T(1024)(128)(2,1)}, u32[]{:S(2)}) copy-start(bf16[1024]{0:T(1024)(128)(2,1)} %get-tuple-element.110) | copy-start | bytes 6148
  823.9 8.9 copy-start.22
  837.2 486.4 %all-reduce.14.cloned.1.call-start = ((), (), s32[]{:S(2)}) async-start(), calls=%async_computation.14 | async-start | bytes 12582912 | tf_op jit(solution)/shard_map/psum | solution.py:362
  1323.6 5.7 copy-start.20
  1323.6 8.2 copy-start.19
  (17 other events, 41.3 us)
Sparse Core Ops, SparseCore 0:
  9.7 120.2 all-gather.12
  131.5 44.1 all-gather.14
  177.3 148.3 all-gather.16
  327.1 147.8 all-gather.18
  544.1 42.0 reduce-scatter.9
  725.2 172.5 reduce-scatter.7
  900.3 144.9 reduce-scatter.11
  1047.8 145.1 reduce-scatter.13
  1195.3 19.8 reduce-scatter.5
  1219.9 103.7 all-reduce.13
where the time goes:
time: 1350 us; the launch traced here: 1340 us
  waiting for transfers between devices  600 us (44%)
  matrix products  347 us (26%)
  blocking collectives  150 us (11%)
  local copies, waits for them, and re-layouts  124 us (9%)
  other arithmetic  78.1 us (6%)
  loops' own time  22.1 us (2%)
  between operations  20 us (1%)
    reduce_scatter x1, waiting for transfers between devices, per_device(): lax.psum_scatter(grads[2].astype(jnp.bfloat16), 'fsdp', scatter_dimension...  145 us
    reduce_scatter x1, waiting for transfers between devices, per_device(): lax.psum_scatter(grads[3].astype(jnp.bfloat16), 'fsdp', scatter_dimension...  144 us
    all_gather x1, waiting for transfers between devices, per_device(): lax.all_gather(hidden_weight, 'fsdp', axis=0, tiled=True)  79.2 us
    all_gather x1, waiting for transfers between devices, per_device(): lax.all_gather(return_weight, 'fsdp', axis=0, tiled=True)  78.7 us
    psum x1, waiting for transfers between devices, per_device(): lax.psum(shortened(tuple((piece * factor for piece in shares))), 'dp')  75.9 us
    dot_general x1, matrix products, per_device(): jnp.dot(second_low, hidden_full, preferred_element_type=jnp.float32)  70.6 us
    reduce_scatter x1, waiting for transfers between devices, per_device(): lax.psum_scatter(grads[0].astype(jnp.bfloat16), 'fsdp', scatter_dimension...  58.6 us
    dot_general x1, matrix products, per_device(): jnp.einsum('rd,fd->rf', output_grad, return_back, preferred_element_type=...  32.7 us
  transfers between devices with their start and end apart: 10, of which 7 were waited for; matrix products, arithmetic and copies ran while one was open for 34% of the time, Pallas kernels for 0%

commit v1 on v0

--- a/solution.py
+++ b/solution.py
@@ -14,6 +14,19 @@
 LARGE_LEN = 145
 ROWS = 1450
 EPS = 1e-06
+
+
+def ring_gather(x, axis, dim):
+    ways = lax.axis_size(axis)
+    up = [(d, (d + 1) % ways) for d in range(ways)]
+    down = [(d, (d - 1) % ways) for d in range(ways)]
+    earlier, later = ([x], [x])
+    for _ in range(ways // 2):
+        earlier.append(lax.ppermute(earlier[-1], axis, up))
+    for _ in range((ways - 1) // 2):
+        later.append(lax.ppermute(later[-1], axis, down))
+    line = jnp.concatenate([*earlier[::-1], *later[1:]], axis=dim)
+    return jnp.roll(line, (lax.axis_index(axis) - ways // 2) * x.shape[dim], axis=dim)
 
 
 def shortened(value):
@@ -145,7 +158,7 @@
         lax.all_gather(input_proj, "fsdp", axis=0, tiled=True),
         lax.all_gather(output_proj, "fsdp", axis=0, tiled=True),
         lax.all_gather(hidden_weight, "fsdp", axis=0, tiled=True),
-        lax.all_gather(return_weight, "fsdp", axis=0, tiled=True),
+        ring_gather(return_weight, "fsdp", 0),
         lax.all_gather(first_gain, "fsdp", axis=0, tiled=True),
         lax.all_gather(first_shift, "fsdp", axis=0, tiled=True),
         lax.all_gather(query_bias, "fsdp", axis=0, tiled=True),

time: 1350 us -> 1450 us (1.074)
  blocking collectives: 150 us -> 299 us
  waiting for transfers between devices: 600 us -> 515 us
  local copies, waits for them, and re-layouts: 124 us -> 146 us
    all_gather x1, blocking collectives: 7.88 us -> 157 us  [per_device(): lax.all_gather(return_bias, 'fsdp', axis=0, tiled=True)]
    reduce_scatter x1, waiting for transfers between devices: 145 us -> 47.1 us  [per_device(): lax.psum_scatter(grads[2].astype(jnp.bfloat16), 'fsdp', scatter_dimension...]
    ppermute x0 -> x3, waiting for transfers between devices: none -> 72.6 us  [the longest x2 72.6 us: ring_gather(): earlier.append(lax.ppermute(earlier[-1], axis, up))]
    reduce_scatter x1, waiting for transfers between devices: 58.6 us -> 0.01 us  [per_device(): lax.psum_scatter(grads[0].astype(jnp.bfloat16), 'fsdp', scatter_dimension...]
    unnamed x113 -> x122, local copies, waits for them, and re-layouts: 10.9 us -> 30.3 us
  transfers between devices with their start and end apart: 10 -> 13, of which waited for: 7 -> 7; matrix products, arithmetic and copies ran while one was open for 34% -> 33% of each run, Pallas kernels for 0% -> 0%
where the time goes in v1:
time: 1450 us; the launch traced here: 1440 us
  waiting for transfers between devices  515 us (36%)
  matrix products  347 us (24%)
  blocking collectives  299 us (21%)
  local copies, waits for them, and re-layouts  146 us (10%)
  other arithmetic  78.2 us (5%)
  loops' own time  22.2 us (2%)
  between operations  19.7 us (1%)
    all_gather x1, blocking collectives, per_device(): lax.all_gather(return_bias, 'fsdp', axis=0, tiled=True)  157 us
    reduce_scatter x1, waiting for transfers between devices, per_device(): lax.psum_scatter(grads[3].astype(jnp.bfloat16), 'fsdp', scatter_dimension...  144 us
    all_gather x1, waiting for transfers between devices, per_device(): lax.all_gather(hidden_weight, 'fsdp', axis=0, tiled=True)  79.1 us
    all_gather x1, waiting for transfers between devices, per_device(): lax.all_gather(return_weight, 'fsdp', axis=0, tiled=True)  78.7 us
    psum x1, waiting for transfers between devices, per_device(): lax.psum(shortened(tuple((piece * factor for piece in shares))), 'dp')  75.8 us
    ppermute x2, waiting for transfers between devices, ring_gather(): earlier.append(lax.ppermute(earlier[-1], axis, up))  72.6 us
    dot_general x1, matrix products, per_device(): jnp.dot(second_low, hidden_full, preferred_element_type=jnp.float32)  70.6 us
    reduce_scatter x1, waiting for transfers between devices, per_device(): lax.psum_scatter(grads[2].astype(jnp.bfloat16), 'fsdp', scatter_dimension...  47.1 us
  transfers between devices with their start and end apart: 13, of which 7 were waited for; matrix products, arithmetic and copies ran while one was open for 33% of the time, Pallas kernels for 0%

profile of v1, /device:TPU:0, one launch (start us, length us, event | category | flops | bytes accessed | tf_op | source)
XLA Modules:
  0.0 1441.5 jit_solution(767518981834758422)
XLA Ops:
  11.0 12.6 all-gather.6
  31.4 9.9 all-gather.4
  41.2 9.6 all-gather.3
  50.9 8.5 all-gather.2
  59.4 10.3 all-gather.1
  69.7 8.6 all-gather
  78.5 12.1 all_gather.58
  90.6 16.1 %all_gather.47 = bf16[50,1024]{1,0:T(8,128)(2,1)S(1)} all-gather(bf16[50,256]{1,0:T(8,128)(2,1)S(1)} %copy-done.34), channel_id=1, replica_groups=mesh['dp'=8,'fsdp'=4] {'fsdp'}, dimensions={1}, use_global_device_ids=true | all-gather | bytes 128000 | tf_op jit(solution)/shard_map/all_gather | solution.py:171
  114.3 15.7 %all-gather.13.cloned.1.call-done = bf16[1024,3072]{1,0:T(8,128)(2,1)} async-done(((bf16[256,3072]{1,0:T(8,128)(2,1)}), bf16[1024,3072]{1,0:T(8,128)(2,1)}) %all-gather.13.cloned.1.call-update) | async-done | bytes 6291472 | tf_op jit(solution)/shard_map/all_gather | solution.py:158
  130.0 17.2 %fusion.77 = f32[1450,3072]{1,0:T(8,128)} fusion(bf16[1024,3072]{1,0:T(8,128)(2,1)} %all-gather.13.cloned.1.call-done, f32[1450,1024]{1,0:T(8,128)} %copy-done.7, f32[1024]{0:T(1024)S(1)} %bitcast.102, f32[1024]{0:T(1024)S(1)} %bitcast.94, f32[1450]{0:T(1024)S(1)} %add_rsqrt_fusion.1, f32[1450]{0:T(1024)S(1)} %broadcast_multiply_fusion.5), kind=kOutput, calls=%fused_computation.175 | convolution fusion | flops 9130035200 | bytes 30068048 | tf_op jit(solution)/shard_map/dot_general | solution.py:208
  150.3 10.0 fusion.52
  160.4 75.4 %conditional.6 = (f32[1450,16]{0,1:T(8,128)}, bf16[1450,1024]{1,0:T(8,128)(2,1)S(1)}) conditional(s32[]{:T(128)} %convert_element_type.404, (bf16[1450,1024]{1,0:T(8,128)(2,1)}, bf16[1450,1024]{1,0:T(8,128)(2,1)S(1)}, bf16[1450,1024]{1,0:T(8,128)(2,1)}) %tuple.44, (bf16[1450,1024]{1,0:T(8,128)(2,1)}, bf16[1450,1024]{1,0:T(8,128)(2,1)S(1)}, ...), branch_computations={%region_3.6_spmd, %region_6.9_spmd} | conditional | flops 889557632 | bytes 82963216
  160.4 9.1 reshape.396
  175.7 14.3 multiply_reduce_fusion
  190.0 8.9 exponential_reduce_fusion
  206.3 8.9 fusion.6
  218.6 7.8 convert_element_type.297
  246.5 79.1 %all-gather.17.cloned.1.call-done = bf16[1024,4096]{1,0:T(8,128)(2,1)} async-done(((bf16[256,4096]{1,0:T(8,128)(2,1)}), bf16[1024,4096]{1,0:T(8,128)(2,1)}) %all-gather.17.cloned.1.call-update) | async-done | bytes 8388624 | tf_op jit(solution)/shard_map/all_gather | solution.py:160
  325.7 70.6 %multiply_convert_fusion.4 = (bf16[1450,4096]{1,0:T(8,128)(2,1)}, f32[1450,4096]{1,0:T(8,128)}, f32[1450,4096]{1,0:T(8,128)}) fusion(f32[4096]{0:T(1024)S(1)} %convert_element_type.416, bf16[1024,4096]{1,0:T(8,128)(2,1)} %all-gather.17.cloned.1.call-done, f32[1450,1024]{1,0:T(8,128)} %copy-done.8, f32[1024]{0:T(1024)S(1)} %bitcast.100, ...), kind=kOutput, calls=%fused_computation.59 | convolution fusion | flops 12562892800 | bytes 73755984 | tf_op jit(solution)/shard_map/dot_general | solution.py:229
  396.3 78.7 %all-gather.19.cloned.1.call-done = bf16[4096,1024]{1,0:T(8,128)(2,1)} async-done(((bf16[1024,1024]{1,0:T(8,128)(2,1)}), bf16[4096,1024]{1,0:T(8,128)(2,1)}) %all-gather.19.cloned.1.call-update) | async-done | bytes 8388624 | tf_op jit(solution)/shard_map/all_gather | solution.py:242
  475.0 32.7 %fusion.84 = (bf16[4096]{0:T(1024)(128)(2,1)}, bf16[1450,4096]{1,0:T(8,128)(2,1)}) fusion(f32[1450,4096]{1,0:T(8,128)} %get-tuple-element.140, bf16[1450,1024]{1,0:T(8,128)(2,1)} %param.24, bf16[4096,1024]{1,0:T(8,128)(2,1)} %all-gather.19.cloned.1.call-done, f32[1450,4096]{1,0:T(8,128)} %get-tuple-element.158, f32[4096]{0:T(1024)S(1)} %convert_element_type.416), kind=kOutput, calls=%fused_computation.181 | convolution fusion | flops 12258504704 | bytes 70774784 | tf_op jit(solution)/shard_map/rd,fd->rf/dot_general | solution.py:252
  507.7 22.7 %multiply_reduce_fusion.4 = (bf16[1024]{0:T(1024)(128)(2,1)}, f32[1450]{0:T(1024)S(1)}, f32[1450]{0:T(1024)S(1)}, bf16[1024]{0:T(1024)(128)(2,1)}, f32[1450,1024]{1,0:T(8,128)}) fusion(f32[1450,1024]{1,0:T(8,128)S(1)} %copy-done.9, f32[1450]{0:T(1024)S(1)} %add_rsqrt_fusion, f32[1450]{0:T(1024)S(1)} %broadcast_multiply_fusion.4, f32[1024]{0:T(1024)S(1)} %bitcast.91, ...), kind=kOutput, calls=%fused_computation.83 | convolution fusion | flops 12176840704 | bytes 32176800 | tf_op jit(solution)/shard_map/rf,df->rd/dot_general | solution.py:260
  544.0 8.4 convolution_convert_fusion.4
  552.4 154.3 %conditional.7 = (bf16[1450,1024]{1,0:T(8,128)(2,1)S(1)}, bf16[1450,1024]{1,0:T(8,128)(2,1)}, bf16[1450,1024]{1,0:T(8,128)(2,1)}) conditional(s32[]{:T(128)} %convert_element_type.404, (bf16[1450,1024]{1,0:T(8,128)(2,1)}, bf16[1450,1024]{1,0:T(8,128)(2,1)S(1)}, f32[1450,16]{0,1:T(8,128)S(1)}, bf16[1450,1024]{1,0:T(8,128)(2,1)}, ...), branch_computations={%region_13.15_spmd, %region_15.17_spmd} | conditional | flops 2199244032 | bytes 259700960
  552.8 8.7 reshape.404
  567.7 9.3 reshape.407
  583.4 13.5 subtract_exponential_fusion
  596.9 8.4 convolution_bitcast_fusion
  608.7 8.9 reshape.410
  617.6 14.3 multiply_reduce_fusion.2
  631.9 9.8 multiply_convert_fusion.1
  644.5 9.1 fusion.29
  653.7 11.1 multiply_bitcast_fusion
  685.1 8.9 convert_element_type.306
  706.8 18.2 %convolution_convert_fusion.3 = bf16[1024,3072]{1,0:T(8,128)(2,1)} fusion(bf16[1450,1024]{1,0:T(8,128)(2,1)} %get-tuple-element.93, bf16[1450,1024]{1,0:T(8,128)(2,1)} %get-tuple-element.92, bf16[1450,1024]{1,0:T(8,128)(2,1)S(1)} %get-tuple-element.91, f32[1450,1024]{1,0:T(8,128)} %copy-done.7, f32[1024]{0:T(1024)S(1)} %bitcast.103, f32[1024]{0:T(1024)S(1)} %bitcast.95, ...), kind=kOutput, calls=%fused_computation.96 | convolution fusion | flops 9159907328 | bytes 21159248 | tf_op jit(solution)/shard_map/rd,re->de/dot_general | solution.py:287
  725.7 21.0 %convolution_convert_fusion.1 = bf16[1024,4096]{1,0:T(8,128)(2,1)} fusion(bf16[1450,4096]{1,0:T(8,128)(2,1)} %get-tuple-element.162, f32[1450,1024]{1,0:T(8,128)} %copy-done.8, f32[1024]{0:T(1024)S(1)} %bitcast.101, f32[1024]{0:T(1024)S(1)} %bitcast.93, f32[1450]{0:T(1024)S(1)} %copy-done.33, f32[1450]{0:T(1024)S(1)} %copy-done.29), kind=kOutput, calls=%fused_computation.76 | convolution fusion | flops 12175099904 | bytes 26226000 | tf_op jit(solution)/shard_map/rd,rf->df/dot_general | solution.py:256
  748.5 18.4 %convolution_convert_fusion.2 = bf16[4096,1024]{1,0:T(8,128)(2,1)} fusion(bf16[1450,4096]{1,0:T(8,128)(2,1)} %get-tuple-element.139, bf16[1450,1024]{1,0:T(8,128)(2,1)S(1)} %copy-done.18), kind=kOutput, calls=%fused_computation.77 | convolution fusion | flops 12167675904 | bytes 23236608 | tf_op jit(solution)/shard_map/rf,rd->fd/dot_general | solution.py:248
  768.5 72.6 %collective-permute-done = bf16[1024,1024]{1,0:T(8,128)(2,1)} collective-permute-done((bf16[1024,1024]{1,0:T(8,128)(2,1)S(1)}, bf16[1024,1024]{1,0:T(8,128)(2,1)}, u32[]{:S(2)}, u32[]{:S(2)}) %collective-permute-start) | collective-permute-done | bytes 2097184 | tf_op jit(solution)/shard_map/ppermute | solution.py:25
  841.0 12.8 collective-permute-start.1
  859.5 156.6 %all-gather.7 = bf16[4,1,256]{2,1,0:T(2,128)(2,1)S(1)} all-gather(bf16[1,1,256]{2,1,0:T(2,128)(2,1)S(1)} %reshape.432), channel_id=1, replica_groups=mesh['dp'=8,'fsdp'=4] {'fsdp'}, dimensions={0}, use_global_device_ids=true | all-gather | bytes 2560 | tf_op jit(solution)/shard_map/all_gather | solution.py:170
  1040.9 18.3 %multiply_reduce_fusion.5 = (bf16[1024]{0:T(1024)(128)(2,1)S(1)}, f32[1450]{0:T(1024)S(1)}, f32[1450]{0:T(1024)S(1)}, bf16[1024]{0:T(1024)(128)(2,1)S(1)}, f32[1450,1024]{1,0:T(8,128)}) fusion(f32[1450,1024]{1,0:T(8,128)} %copy-done.7, f32[1450]{0:T(1024)S(1)} %copy-done.31, f32[1450]{0:T(1024)S(1)} %copy-done.27, f32[1024]{0:T(1024)S(1)} %bitcast.96, ...), kind=kOutput, calls=%fused_computation.84 | convolution fusion | flops 9162696704 | bytes 27110048 | tf_op jit(solution)/shard_map/re,de->rd/dot_general | solution.py:292
  1059.2 20.8 %all-reduce.11 = (bf16[1024]{0:T(1024)(128)(2,1)S(1)}, bf16[1024]{0:T(1024)(128)(2,1)S(1)}, bf16[1024]{0:T(1024)(128)(2,1)S(1)}, bf16[1024]{0:T(1024)(128)(2,1)S...) all-reduce(bf16[1024]{0:T(1024)(128)(2,1)S(1)} %get-tuple-element.1, ...), channel_id=3, replica_groups=mesh['dp'=8,'fsdp'=4] {'fsdp'}, use_global_device_ids=true, to_apply=%region_22.23.clone | all-reduce | flops 12288 | bytes 49152
  1080.6 9.0 fusion.79
  1099.1 47.1 %reduce-scatter.12.cloned.1.call-done = bf16[256,4096]{1,0:T(8,128)(2,1)} async-done(((bf16[1024,4096]{1,0:T(8,128)(2,1)}), bf16[256,4096]{1,0:T(8,128)(2,1)}) %reduce-scatter.12.cloned.1.call-update) | async-done | bytes 2097168 | tf_op jit(solution)/shard_map/reduce_scatter | solution.py:336
  1149.5 143.8 %reduce-scatter.14.cloned.1.call-done = bf16[1024,1024]{1,0:T(8,128)(2,1)} async-done(((bf16[4096,1024]{1,0:T(8,128)(2,1)}), bf16[1024,1024]{1,0:T(8,128)(2,1)}) %reduce-scatter.14.cloned.1.call-update) | async-done | bytes 2097168 | tf_op jit(solution)/shard_map/reduce_scatter | solution.py:339
  1296.7 19.1 %add_convert_fusion.1 = bf16[1450,1024]{1,0:T(8,128)(2,1)} fusion(f32[1450,1024]{1,0:T(8,128)} %copy-done.8, bf16[1450,4096]{1,0:T(8,128)(2,1)} %get-tuple-element.139, bf16[8192,1024]{1,0:T(8,128)(2,1)} %constant_dynamic-update-slice_fusion, s32[]{:T(128)S(6)} %select_n.212, f32[1024]{0:T(1024)S(1)} %bitcast.104), kind=kOutput, calls=%fused_computation.89 | convolution fusion | flops 12167936000 | bytes 29253636 | tf_op jit(solution)/shard_map/dot_general | solution.py:234
  1316.5 25.7 %all-reduce.9 = (bf16[50,256]{1,0:T(8,128)(2,1)S(1)}, bf16[256]{0:T(256)(128)(2,1)S(1)}, bf16[256]{0:T(256)(128)(2,1)S(1)}, bf16[256]{0:T(256)(128)(2,1)S(1)}, b...) all-reduce(bf16[50,256]{1,0:T(8,128)(2,1)S(1)} %multiply_convert_fu, ...), channel_id=1, replica_groups=mesh['dp'=8,'fsdp'=4] {'dp'}, use_global_device_ids=true, to_apply=%region_20.21 | all-reduce | flops 15872 | bytes 63488 | tf_op jit(solution)/shard_map/psum | solution.py:375
  1348.0 75.8 %all-reduce.14.cloned.1.call-done = (bf16[256,3072]{1,0:T(8,128)(2,1)}, bf16[256,1024]{1,0:T(8,128)(2,1)}, bf16[256,4096]{1,0:T(8,128)(2,1)}, bf16[1024,1024]{1,0:T(8,128)(2,1)}) async-done(((bf16[256,3072]{1,0:T(8,128)(2,1)}, bf16[256,1024]{1,0:T(8,128)(2,1)}, bf16[256,4096]{1,0:T(8,128)(2,1)}, bf16[1024,1024]{1,0:T(8,128)(2,1)}), (bf16[256,3072]{1,0:T(8,128)(2,1)}, bf16[256,1024]{1,0:T(8,128)(2,1)}, ...) | async-done | bytes 6291472 | tf_op jit(solution)/shard_map/psum | solution.py:375
  (237 shorter events, 166.5 us)
Async XLA Ops:
  7.3 71.3 %copy-start.47 = (bf16[1024]{0:T(1024)(128)(2,1)S(1)}, bf16[1024]{0:T(1024)(128)(2,1)}, u32[]{:S(2)}) copy-start(bf16[1024]{0:T(1024)(128)(2,1)} %param.39) | copy-start | bytes 6148
  7.3 83.3 %copy-start.34 = (bf16[50,256]{1,0:T(8,128)(2,1)S(1)}, bf16[50,256]{1,0:T(8,128)(2,1)}, u32[]{:S(2)}) copy-start(bf16[50,256]{1,0:T(8,128)(2,1)} %param.28) | copy-start | bytes 76804
  7.3 99.5 %copy-start.42 = (s32[145,4]{0,1:T(4,128)S(1)}, s32[145,4]{0,1:T(4,128)}, u32[]{:S(2)}) copy-start(s32[145,4]{0,1:T(4,128)} %param.27) | copy-start | bytes 6964
  7.3 100.5 %copy-start.19 = (bf16[1450,1024]{1,0:T(8,128)(2,1)S(1)}, bf16[1450,1024]{1,0:T(8,128)(2,1)}, u32[]{:S(2)}) copy-start(bf16[1450,1024]{1,0:T(8,128)(2,1)} %param.23) | copy-start | bytes 8908804
  7.3 122.7 %all-gather.13.cloned.1.call-start = ((), (), s32[]{:S(2)}) async-start(), calls=%async_computation.5 | async-start | bytes 7864320 | tf_op jit(solution)/shard_map/all_gather | solution.py:158
  8.0 227.7 %all-gather.15.cloned.1.call-start = ((), (), s32[]{:S(2)}) async-start(), calls=%async_computation.6 | async-start | bytes 2621440 | tf_op jit(solution)/shard_map/all_gather | solution.py:159
  8.8 316.9 %all-gather.17.cloned.1.call-start = ((), (), s32[]{:S(2)}) async-start(), calls=%async_computation.7 | async-start | bytes 10485760 | tf_op jit(solution)/shard_map/all_gather | solution.py:160
  9.5 465.5 %all-gather.19.cloned.1.call-start = ((), (), s32[]{:S(2)}) async-start(), calls=%async_computation.8 | async-start | bytes 10485760 | tf_op jit(solution)/shard_map/all_gather | solution.py:242
  10.1 1084.1 %reduce-scatter.10.cloned.1.call-start = ((), (), s32[]{:S(2)}) async-start(), calls=%async_computation.11 | async-start | bytes 2621440 | tf_op jit(solution)/shard_map/reduce_scatter | solution.py:333
  23.7 302.0 %copy-start.43 = (f32[4,1,256]{2,1,0:T(1,128)}, f32[4,1,256]{2,1,0:T(1,128)S(1)}, u32[]{:S(2)}) copy-start(f32[4,1,256]{2,1,0:T(1,128)S(1)} %convert_element_type.486) | copy-start | bytes 12292
  31.4 499.1 %copy-start.35 = (f32[4,1,256]{2,1,0:T(1,128)}, f32[4,1,256]{2,1,0:T(1,128)S(1)}, u32[]{:S(2)}) copy-start(f32[4,1,256]{2,1,0:T(1,128)S(1)} %convert_element_type.485) | copy-start | bytes 12292
  69.7 60.2 %copy-start.45 = (f32[4,1,256]{2,1,0:T(1,128)}, f32[4,1,256]{2,1,0:T(1,128)S(1)}, u32[]{:S(2)}) copy-start(f32[4,1,256]{2,1,0:T(1,128)S(1)} %convert_element_type.481) | copy-start | bytes 12292
  78.4 51.6 %copy-start.37 = (f32[4,1,256]{2,1,0:T(1,128)}, f32[4,1,256]{2,1,0:T(1,128)S(1)}, u32[]{:S(2)}) copy-start(f32[4,1,256]{2,1,0:T(1,128)S(1)} %convert_element_type.480) | copy-start | bytes 12292
  111.0 19.0 %copy-start.26 = (f32[1450]{0:T(1024)}, f32[1450]{0:T(1024)S(1)}, u32[]{:S(2)}) copy-start(f32[1450]{0:T(1024)S(1)} %broadcast_multiply_fusion.5) | copy-start | bytes 17404
  114.3 15.7 %copy-start.30 = (f32[1450]{0:T(1024)}, f32[1450]{0:T(1024)S(1)}, u32[]{:S(2)}) copy-start(f32[1450]{0:T(1024)S(1)} %add_rsqrt_fusion.1) | copy-start | bytes 17404
  150.3 10.0 copy-start.1
  190.0 10.0 copy-start.3
  243.3 287.1 %copy-start.28 = (f32[1450]{0:T(1024)}, f32[1450]{0:T(1024)S(1)}, u32[]{:S(2)}) copy-start(f32[1450]{0:T(1024)S(1)} %broadcast_multiply_fusion.4) | copy-start | bytes 17404
  246.5 283.9 %copy-start.32 = (f32[1450]{0:T(1024)}, f32[1450]{0:T(1024)S(1)}, u32[]{:S(2)}) copy-start(f32[1450]{0:T(1024)S(1)} %add_rsqrt_fusion) | copy-start | bytes 17404
  475.0 32.7 %copy-start.9 = (f32[1450,1024]{1,0:T(8,128)S(1)}, f32[1450,1024]{1,0:T(8,128)}, u32[]{:S(2)}) copy-start(f32[1450,1024]{1,0:T(8,128)} %copy-done.8) | copy-start | bytes 17817604
  507.7 22.8 %copy-start.17 = (bf16[1450,1024]{1,0:T(8,128)(2,1)S(1)}, bf16[1450,1024]{1,0:T(8,128)(2,1)}, u32[]{:S(2)}) copy-start(bf16[1450,1024]{1,0:T(8,128)(2,1)} %param.24) | copy-start | bytes 8908804
  530.5 8.7 copy-start.16
  543.9 8.5 copy-start.2
  543.9 8.4 copy-start.24
  543.9 552.3 %reduce-scatter.8.cloned.1.call-start = ((), (), s32[]{:S(2)}) async-start(), calls=%async_computation.10 | async-start | bytes 7864320 | tf_op jit(solution)/shard_map/reduce_scatter | solution.py:330
  552.4 154.4 %copy-start.27 = (f32[1450]{0:T(1024)S(1)}, f32[1450]{0:T(1024)}, u32[]{:S(2)}) copy-start(f32[1450]{0:T(1024)} %copy-done.26) | copy-start | bytes 17404
  552.4 154.4 %copy-start.31 = (f32[1450]{0:T(1024)S(1)}, f32[1450]{0:T(1024)}, u32[]{:S(2)}) copy-start(f32[1450]{0:T(1024)} %copy-done.30) | copy-start | bytes 17404
  552.4 154.4 %copy-start.38 = (f32[4,1,256]{2,1,0:T(1,128)S(1)}, f32[4,1,256]{2,1,0:T(1,128)}, u32[]{:S(2)}) copy-start(f32[4,1,256]{2,1,0:T(1,128)} %copy-done.37) | copy-start | bytes 12292
  552.4 154.4 %copy-start.46 = (f32[4,1,256]{2,1,0:T(1,128)S(1)}, f32[4,1,256]{2,1,0:T(1,128)}, u32[]{:S(2)}) copy-start(f32[4,1,256]{2,1,0:T(1,128)} %copy-done.45) | copy-start | bytes 12292
  567.7 9.3 copy-start.4
  706.7 18.2 %copy-start.14 = (bf16[1450,1024]{1,0:T(8,128)(2,1)}, bf16[1450,1024]{1,0:T(8,128)(2,1)S(1)}, u32[]{:S(2)}) copy-start(bf16[1450,1024]{1,0:T(8,128)(2,1)S(1)} %get-tuple-element.91) | copy-start | bytes 8908804
  725.0 421.1 %reduce-scatter.12.cloned.1.call-start = ((), (), s32[]{:S(2)}) async-start(), calls=%async_computation.12 | async-start | bytes 10485760 | tf_op jit(solution)/shard_map/reduce_scatter | solution.py:336
  746.7 546.6 %reduce-scatter.14.cloned.1.call-start = ((), (), s32[]{:S(2)}) async-start(), calls=%async_computation.13 | async-start | bytes 10485760 | tf_op jit(solution)/shard_map/reduce_scatter | solution.py:339
  766.9 87.5 %copy-start.57 = (s32[2]{0:T(128)S(1)}, s32[2]{0:T(128)}, u32[]{:S(2)}) copy-start(s32[2]{0:T(128)} %param.26) | copy-start | bytes 28
  766.9 90.7 %copy-start.59 = (u32[32]{0:T(128)S(1)}, u32[32]{0:T(128)}, u32[]{:S(2)}) copy-start(u32[32]{0:T(128)} %constant.212) | copy-start | bytes 388
  766.9 92.6 %copy-start.58 = (bf16[256]{0:T(256)(128)(2,1)S(1)}, bf16[256]{0:T(256)(128)(2,1)}, u32[]{:S(2)}) copy-start(bf16[256]{0:T(256)(128)(2,1)} %param.41) | copy-start | bytes 1540
  766.9 548.9 %reduce-scatter.6.cloned.1.call-start = ((), (), s32[]{:S(2)}) async-start(), calls=%async_computation.9 | async-start | bytes 143360 | tf_op jit(solution)/shard_map/reduce_scatter | solution.py:369
  768.5 72.6 %collective-permute-start = (bf16[1024,1024]{1,0:T(8,128)(2,1)S(1)}, bf16[1024,1024]{1,0:T(8,128)(2,1)}, u32[]{:S(2)}, u32[]{:S(2)}) collective-permute-start(bf16[1024,1024]{1,0:T(8,128)(2,1)S(1)} %copy-done.11), channel_id=1, source_target_pairs={{0,1},{1,2},{2,3},{3,0},{4,5},{5,6},{6,7},{7,4},{8,9},{9,10},{10,1... | collective-permute-start | bytes 6291464 | tf_op jit(solution)/shard_map/ppermute | solution.py:25
  841.0 175.1 %collective-permute-start.1 = (bf16[1024,1024]{1,0:T(8,128)(2,1)}, bf16[1024,1024]{1,0:T(8,128)(2,1)}, u32[]{:S(2)}, u32[]{:S(2)}) collective-permute-start(bf16[1024,1024]{1,0:T(8,128)(2,1)} %collective-permute-done), channel_id=1, source_target_pairs={{0,1},{1,2},{2,3},{3,0},{4,5},{5,6},{6,7},{7,4},{8,9},{9,10},{10,1... | collective-permute-start | bytes 6291464 | tf_op jit(solution)/shard_map/ppermute | solution.py:25
  853.9 169.9 %collective-permute-start.2 = (bf16[1024,1024]{1,0:T(8,128)(2,1)S(1)}, bf16[1024,1024]{1,0:T(8,128)(2,1)}, u32[]{:S(2)}, u32[]{:S(2)}) collective-permute-start(bf16[1024,1024]{1,0:T(8,128)(2,1)S(1)} %copy-done.11), channel_id=1, source_target_pairs={{0,3},{1,0},{2,1},{3,2},{4,7},{5,4},{6,5},{7,6},{8,11},{9,8},{10,9... | collective-permute-start | bytes 6291464 | tf_op jit(solution)/shard_map/ppermute | solution.py:27
  1040.8 18.3 %copy-start.39 = (bf16[1024]{0:T(1024)(128)(2,1)S(1)}, bf16[1024]{0:T(1024)(128)(2,1)}, u32[]{:S(2)}) copy-start(bf16[1024]{0:T(1024)(128)(2,1)} %get-tuple-element.135) | copy-start | bytes 6148
  1040.8 18.3 %copy-start.40 = (bf16[1024]{0:T(1024)(128)(2,1)S(1)}, bf16[1024]{0:T(1024)(128)(2,1)}, u32[]{:S(2)}) copy-start(bf16[1024]{0:T(1024)(128)(2,1)} %get-tuple-element.151) | copy-start | bytes 6148
  1040.8 18.3 %copy-start.41 = (bf16[4096]{0:T(1024)(128)(2,1)S(1)}, bf16[4096]{0:T(1024)(128)(2,1)}, u32[]{:S(2)}) copy-start(bf16[4096]{0:T(1024)(128)(2,1)} %get-tuple-element.161) | copy-start | bytes 24580
  1040.8 18.3 %copy-start.48 = (bf16[1024]{0:T(1024)(128)(2,1)S(1)}, bf16[1024]{0:T(1024)(128)(2,1)}, u32[]{:S(2)}) copy-start(bf16[1024]{0:T(1024)(128)(2,1)} %get-tuple-element.104) | copy-start | bytes 6148
  1040.8 18.3 %copy-start.49 = (bf16[1024]{0:T(1024)(128)(2,1)S(1)}, bf16[1024]{0:T(1024)(128)(2,1)}, u32[]{:S(2)}) copy-start(bf16[1024]{0:T(1024)(128)(2,1)} %get-tuple-element.110) | copy-start | bytes 6148
  1080.6 9.0 copy-start.23
  1094.0 329.8 %all-reduce.14.cloned.1.call-start = ((), (), s32[]{:S(2)}) async-start(), calls=%async_computation.14 | async-start | bytes 12582912 | tf_op jit(solution)/shard_map/psum | solution.py:375
  1423.8 8.2 copy-start.20
  (21 other events, 64.9 us)
Sparse Core Ops, SparseCore 0:
  9.7 120.2 all-gather.12
  131.5 44.0 all-gather.14
  177.2 148.3 all-gather.16
  327.1 147.8 all-gather.18
  544.0 42.0 reduce-scatter.9
  725.1 273.7 reduce-scatter.7
  1001.4 144.6 reduce-scatter.11
  1148.6 144.5 reduce-scatter.13
  1295.6 19.8 reduce-scatter.5
  1320.1 103.5 all-reduce.13
